TPU v7x, 32 devices: a whole 2x2x4 slice. The times are simulated.
32 devices in a mesh: rec: 8 (over z, core), frame: 4 (over y, x).
Axes of the slice: x: 2, y: 2, z: 4, core: 2. Of those that a mesh axis runs over, the one named last changes fastest.
Arguments:
- frames: bfloat16 [8, 6144, 256], P('rec', 'frame'), may hold values from -10 to 10
- texts: bfloat16 [16, 224, 256], P('rec', 'frame'), may hold values from -100 to 100
- pair_rec: int32 [16, 1], replicated, may hold values from 0 to 7, as said below
- pair_text: int32 [16], replicated, may hold values from 0 to 15, as said below
- pair_label: int32 [16], replicated, may hold values 0 or 1
Outputs:
- loss: float32 [], replicated
- grad_frames: bfloat16 [8, 6144, 256], P('rec', 'frame')
- grad_texts: bfloat16 [16, 224, 256], P('rec', 'frame')
Inputs may be any that keep to these rules, and one draw needn't show every extreme that they name: `pair_rec`: no recording is named by more than 6 pairs, some recording by exactly 6, and every recording by at least one. A pair's text is held by the index of rec one after, one before, or 4 after its recording (counted round): pair_text // 2 = (pair_rec + k) mod 8 with k one of 1, 7, 4.
All inputs are finite; a program needn't handle non-finite values.
Results may differ from a plain program's by a relative error of at most 0.0085.
Values may be sent and summed in bfloat16 or wider, within the bound.
No kernel may reach another device: no remote copies, remote signals or barrier semaphores. Data moves between devices by JAX's collectives and lax.ppermute only.
A program may use at most 64 MiB of HBM per device.

v0:
```python
import jax
import jax.numpy as jnp
from jax import lax
from jax.sharding import PartitionSpec as P

MOST = 6
EPS = 1e-06
TEMP = 10.0
BIAS = -1.0
LOSS_SCALE = 2048.0


def slot_tables(pair_rec, pair_text, pair_label, here, most):
    record = pair_rec[:, 0]
    count = record.shape[0]
    order = jnp.arange(count, dtype=jnp.int32)
    same = (record[:, None] == record[None, :]).astype(jnp.int32)
    earlier = (order[None, :] < order[:, None]).astype(jnp.int32)
    rank = jnp.sum(same * earlier, axis=1)
    places = jnp.arange(most, dtype=jnp.int32)
    chosen = ((record[None, :] == here) & (rank[None, :] == places[:, None])).astype(jnp.int32)
    valid = jnp.sum(chosen, axis=1)
    slot_text = jnp.sum(chosen * pair_text[None, :], axis=1)
    sign = jnp.sum(chosen * (2 * pair_label[None, :] - 1), axis=1)
    return (valid, slot_text, sign)


def pair_terms(score, valid, sign, tokens):
    margin = -sign * (TEMP * score + BIAS)
    loss_part = valid * jax.nn.softplus(margin)
    grad_cos = -LOSS_SCALE * TEMP * valid * sign * jax.nn.sigmoid(margin) / tokens
    return (loss_part, grad_cos)


def body(frames, texts, pair_rec, pair_text, pair_label):
    here = lax.axis_index("rec")
    part = lax.axis_index("frame")
    owned, width_rows, width = texts.shape
    tokens = width_rows * lax.axis_size("frame")
    n_text = owned * lax.axis_size("rec")
    valid, slot_text, sign = slot_tables(pair_rec, pair_text, pair_label, here, MOST)
    valid_f = valid.astype(jnp.float32)
    sign_f = sign.astype(jnp.float32)
    picks = (
        (slot_text[:, None] == jnp.arange(n_text, dtype=jnp.int32)[None, :]) & (valid[:, None] > 0)
    ).astype(jnp.bfloat16)
    local = jnp.einsum(
        "jc,cgx->jgx",
        picks,
        lax.all_gather(texts, "rec", axis=0, tiled=True),
        preferred_element_type=jnp.float32,
    ).astype(jnp.bfloat16)
    query_vectors = lax.all_gather(local, "frame", axis=1, tiled=True)
    upstream_signal = frames[0]
    logit_scale = width ** (-0.5)
    pair_scores = (
        jnp.einsum(
            "ype,je->ypj", query_vectors, upstream_signal, preferred_element_type=jnp.float32
        )
        * logit_scale
    )
    local_max = jnp.max(pair_scores, axis=2)
    row_max = lax.pmax(local_max, "frame")
    expo = jnp.exp(pair_scores - row_max[..., None])
    batch_weights = expo.astype(jnp.bfloat16)
    value_partial = jnp.einsum(
        "pqx,xh->pqh", batch_weights, upstream_signal, preferred_element_type=jnp.float32
    )
    query_f = query_vectors.astype(jnp.float32)
    q_norm = lax.rsqrt(jnp.sum(query_f * query_f, axis=2) + EPS)
    q_unit = query_f * q_norm[..., None]
    context = lax.psum(value_partial, "frame")
    c_norm = lax.rsqrt(jnp.sum(context * context, axis=2) + EPS)
    c_unit = context * c_norm[..., None]
    cos = jnp.sum(q_unit * c_unit, axis=2)
    score = jnp.mean(cos, axis=1)
    loss_part, grad_cos = pair_terms(score, valid_f, sign_f, tokens)
    weight = grad_cos[:, None, None]
    d_context = weight * (q_unit - cos[..., None] * c_unit) * c_norm[..., None]
    direct = weight * (c_unit - cos[..., None] * q_unit) * q_norm[..., None]
    direct_own = lax.dynamic_slice_in_dim(direct, part * width_rows, width_rows, 1)
    context_batch_gradient = d_context.astype(jnp.bfloat16)
    weight_gradient = jnp.einsum(
        "ype,je->ypj", context_batch_gradient, upstream_signal, preferred_element_type=jnp.float32
    )
    score_gradient = (expo * weight_gradient * logit_scale).astype(jnp.bfloat16)
    d_query = lax.psum_scatter(
        jnp.einsum(
            "slf,fd->lsd", score_gradient, upstream_signal, preferred_element_type=jnp.float32
        ),
        "frame",
        scatter_dimension=0,
        tiled=True,
    )
    d_query = d_query + jnp.transpose(direct_own, (1, 0, 2))
    text_term = jnp.einsum(
        "st,lsd->tld", picks.astype(jnp.float32), d_query, precision=lax.Precision.HIGHEST
    )
    grad_texts = lax.psum_scatter(text_term, "rec", scatter_dimension=0, tiled=True).astype(
        jnp.bfloat16
    )
    frame_loss_piece = jnp.einsum(
        "cvm,cvz->mz", score_gradient, query_vectors, preferred_element_type=jnp.float32
    )
    frame_loss_piece = frame_loss_piece + jnp.einsum(
        "cvm,cvz->mz", batch_weights, context_batch_gradient, preferred_element_type=jnp.float32
    )
    grad_frames = frame_loss_piece.astype(jnp.bfloat16)[None]
    loss = lax.psum(jnp.sum(loss_part), "rec")
    return (loss, grad_frames, grad_texts)


def solution(mesh):
    return jax.shard_map(
        body,
        mesh=mesh,
        in_specs=(P("rec", "frame", None), P("rec", "frame", None), P(), P(), P()),
        out_specs=(P(), P("rec", "frame", None), P("rec", "frame", None)),
        check_vma=False,
    )
```

profile of v0, /device:TPU:0, one launch (start us, length us, event | category | flops | bytes accessed | tf_op | source)
XLA Modules:
  0.0 205.2 jit_solution(4087020698551283832)
XLA Ops:
  7.2 0.0 copy-start
  7.2 0.0 all-reduce.2.cloned.1.call-start
  7.2 0.7 multiply_add_fusion
  8.0 0.7 broadcast_compare_fusion.1
  8.6 0.9 select_reduce_fusion
  9.5 0.8 select_reduce_fusion.2
  10.3 0.0 copy-start.8
  10.4 0.0 copy-start.9
  10.4 16.6 %all_gather.6 = bf16[16,56,256]{2,1,0:T(8,128)(2,1)S(1)} all-gather(bf16[2,56,256]{2,1,0:T(8,128)(2,1)} %param.6), channel_id=1, replica_groups=mesh['rec'=8,'frame'=4] {'rec'}, dimensions={0}, use_global_device_ids=true | all-gather | bytes 516096 | tf_op jit(solution)/shard_map/all_gather | solution.py:50
  27.0 0.0 copy-done.8
  27.0 0.0 copy-done.9
  27.0 0.3 convolution_convert_fusion
  27.3 12.4 %all_gather.7 = bf16[6,224,256]{2,1,0:T(8,128)(2,1)S(1)} all-gather(bf16[6,56,256]{2,1,0:T(8,128)(2,1)S(1)} %copy.20), channel_id=1, replica_groups=mesh['rec'=8,'frame'=4] {'frame'}, dimensions={1}, use_global_device_ids=true | all-gather | bytes 860160 | tf_op jit(solution)/shard_map/all_gather | solution.py:53
  39.7 0.0 copy-done
  39.7 4.4 %multiply_reduce_fusion = (f32[6,224]{1,0:T(8,128)S(1)}, f32[6,224,1536]{2,1,0:T(8,128)}) fusion(bf16[6,224,256]{2,1,0:T(8,128)(2,1)S(1)} %all_gather.7, bf16[1,1536,256]{2,1,0:T(8,128)(2,1)S(1)} %copy-done), kind=kOutput, calls=%fused_computation.2 | convolution fusion | flops 1061092032 | bytes 9737472 | tf_op jit(solution)/shard_map/ype,je->ypj/dot_general | solution.py:57
  44.1 9.1 %pmax.7 = f32[6,224]{1,0:T(8,128)S(1)} all-reduce(f32[6,224]{1,0:T(8,128)S(1)} %get-tuple-element.16), channel_id=1, replica_groups=mesh['rec'=8,'frame'=4] {'frame'}, use_global_device_ids=true, to_apply=%region_6.0 | all-reduce | flops 1344 | bytes 10752 | tf_op jit(solution)/shard_map/pmax | solution.py:63
  53.2 0.0 copy-start.4
  53.2 6.0 %fusion.7 = f32[6,224,256]{2,1,0:T(8,128)} fusion(bf16[1,1536,256]{2,1,0:T(8,128)(2,1)S(1)} %copy-done, f32[6,224,1536]{2,1,0:T(8,128)} %get-tuple-element.17, f32[6,224]{1,0:T(8,128)S(1)} %pmax.7), kind=kOutput, calls=%fused_computation.18 | convolution fusion | flops 1063157760 | bytes 10425600 | tf_op jit(solution)/shard_map/pqx,xh->pqh/dot_general | solution.py:66
  59.2 0.0 copy-done.4
  59.2 0.0 all-reduce.2.cloned.1.call-update
  59.2 0.0 reduce-scatter.3.cloned.1.call-start
  59.3 0.3 fusion.4
  59.6 57.4 %all-reduce.2.cloned.1.call-done = f32[6,224,256]{2,1,0:T(8,128)} async-done(((f32[6,224,256]{2,1,0:T(8,128)}), f32[6,224,256]{2,1,0:T(8,128)}) %all-reduce.2.cloned.1.call-update) | async-done | bytes 1376272 | tf_op jit(solution)/shard_map/psum | solution.py:72
  116.9 0.0 copy-start.1
  116.9 1.8 multiply_reduce_fusion.1
  118.7 0.0 copy-start.5
  118.7 2.9 %multiply_reduce_fusion.2 = (f32[6,224]{1,0:T(8,128)S(1)}, f32[6]{0:T(128)S(1)}, f32[6,224,256]{2,1,0:T(8,128)S(1)}) fusion(f32[6,224]{1,0:T(8,128)S(1)} %add_rsqrt_fusion.1, bf16[6,224,256]{2,1,0:T(8,128)(2,1)S(1)} %all_gather.7, f32[6,224,256]{2,1,0:T(8,128)} %all-reduce.2.cloned.1.call-done, f32[6,224]{1,0:T(8,128)S(1)} %add_rsqrt_fusion), kind=kLoop, calls=%fused_computation.23 | loop fusion | flops 2063034 | bytes 3456792 | tf_op jit(solution)/shard_map/reduce_sum | solution.py:75
  121.6 0.6 fusion.31
  122.3 0.0 copy-start.7
  122.3 1.6 convert_multiply_fusion
  123.9 0.0 copy-done.7
  123.9 0.0 copy-done.1
  123.9 0.0 copy-done.5
  123.9 2.3 %multiply_convert_fusion = bf16[6,224,1536]{2,1,0:T(8,128)(2,1)S(1)} fusion(f32[6,224,1536]{2,1,0:T(8,128)S(1)} %copy-done.1, bf16[6,224,256]{2,1,0:T(8,128)(2,1)S(1)} %get-tuple-element.13, f32[6,224]{1,0:T(8,128)S(1)} %copy-done.5, bf16[1,1536,256]{2,1,0:T(8,128)(2,1)S(1)} %copy-done), kind=kOutput, calls=%fused_computation | convolution fusion | flops 1067286528 | bytes 13866240 | tf_op jit(solution)/shard_map/ype,je->ypj/dot_general | solution.py:83
  126.2 0.0 copy-start.2
  126.2 2.0 copy-done.2
  128.2 2.3 %convolution_bitcast_fusion.2 = f32[224,6,256]{2,0,1:T(8,128)} fusion(bf16[6,224,1536]{2,1,0:T(8,128)(2,1)S(1)} %multiply_convert_fusion, bf16[1,1536,256]{2,1,0:T(8,128)(2,1)S(1)} %copy-done), kind=kOutput, calls=%fused_computation.11 | convolution fusion | flops 1056964608 | bytes 6291456 | tf_op jit(solution)/shard_map/slf,fd->lsd/dot_general | solution.py:88
  130.5 0.0 reduce-scatter.3.cloned.1.call-update
  130.5 0.0 reduce-scatter.5.cloned.1.call-start
  130.6 0.7 constant_dynamic-slice_fusion
  131.2 0.0 copy-start.6
  131.2 0.7 constant_dynamic-slice_fusion.1
  131.9 28.7 %reduce-scatter.3.cloned.1.call-done = f32[56,6,256]{2,0,1:T(8,128)} async-done(((f32[224,6,256]{2,0,1:T(8,128)}), f32[56,6,256]{2,0,1:T(8,128)}) %reduce-scatter.3.cloned.1.call-update) | async-done | bytes 344080 | tf_op jit(solution)/shard_map/reduce_scatter | solution.py:87
  160.5 1.2 fusion.19
  161.8 1.4 fusion.13
  163.2 1.5 copy.22
  164.7 0.0 reduce-scatter.5.cloned.1.call-update
  164.7 17.1 %psum.15 = f32[]{:T(128)} all-reduce(f32[]{:T(128)} %get-tuple-element.15), channel_id=1, replica_groups=mesh['rec'=8,'frame'=4] {'rec'}, use_global_device_ids=true, to_apply=%region_11.12 | all-reduce | flops 1 | bytes 8 | tf_op jit(solution)/shard_map/psum | solution.py:109
  181.8 0.0 copy-done.6
  181.8 0.0 copy-start.3
  181.8 5.5 %convolution_bitcast_fusion = f32[1536,256]{1,0:T(8,128)S(1)} fusion(bf16[6,224,256]{2,1,0:T(8,128)(2,1)S(1)} %get-tuple-element.13, f32[6,224,1536]{2,1,0:T(8,128)} %get-tuple-element.17, f32[6,224]{1,0:T(8,128)S(1)} %copy-done.6), kind=kOutput, calls=%fused_computation.4 | convolution fusion | flops 1063157760 | bytes 10523904 | tf_op jit(solution)/shard_map/cvm,cvz->mz/dot_general | solution.py:105
  187.3 0.0 copy-done.3
  187.3 2.4 %fusion.3 = bf16[1,1536,256]{2,1,0:T(8,128)(2,1)} fusion(f32[1536,256]{1,0:T(8,128)S(1)} %convolution_bitcast_fusion, bf16[6,224,1536]{2,1,0:T(8,128)(2,1)S(1)} %copy-done.3, bf16[6,224,256]{2,1,0:T(8,128)(2,1)S(1)} %all_gather.7), kind=kOutput, calls=%fused_computation.8 | convolution fusion | flops 1057751040 | bytes 7176192 | tf_op jit(solution)/shard_map/cvm,cvz->mz/dot_general | solution.py:102
  189.7 7.5 %reduce-scatter.5.cloned.1.call-done = f32[2,56,256]{2,1,0:T(8,128)} async-done(((f32[16,56,256]{2,1,0:T(8,128)}), f32[2,56,256]{2,1,0:T(8,128)}) %reduce-scatter.5.cloned.1.call-update) | async-done | bytes 114704 | tf_op jit(solution)/shard_map/reduce_scatter | solution.py:99
  197.1 1.5 convert_element_type.54
  (4 shorter events, 0.0 us)
Async XLA Ops:
  7.2 32.5 %copy-start = (bf16[1,1536,256]{2,1,0:T(8,128)(2,1)S(1)}, bf16[1,1536,256]{2,1,0:T(8,128)(2,1)}, u32[]{:S(2)}) copy-start(bf16[1,1536,256]{2,1,0:T(8,128)(2,1)} %param.5) | copy-start | bytes 2359300
  7.2 109.8 %all-reduce.2.cloned.1.call-start = ((), (), s32[]{:S(2)}) async-start(), calls=%async_computation.2 | async-start | bytes 2752512 | tf_op jit(solution)/shard_map/psum | solution.py:72
  10.3 16.6 %copy-start.8 = (s32[6]{0:T(128)}, s32[6]{0:T(128)S(1)}, u32[]{:S(2)}) copy-start(s32[6]{0:T(128)S(1)} %get-tuple-element.9) | copy-start | bytes 76
  10.4 16.6 %copy-start.9 = (pred[6]{0:T(512)(128)(4,1)}, pred[6]{0:T(512)(128)(4,1)S(1)}, u32[]{:S(2)}) copy-start(pred[6]{0:T(512)(128)(4,1)S(1)} %broadcast_compare_fusion) | copy-start | bytes 22
  53.2 6.0 %copy-start.4 = (f32[6,224]{1,0:T(8,128)}, f32[6,224]{1,0:T(8,128)S(1)}, u32[]{:S(2)}) copy-start(f32[6,224]{1,0:T(8,128)S(1)} %pmax.7) | copy-start | bytes 16132
  59.2 101.3 %reduce-scatter.3.cloned.1.call-start = ((), (), s32[]{:S(2)}) async-start(), calls=%async_computation.3 | async-start | bytes 1720320 | tf_op jit(solution)/shard_map/reduce_scatter | solution.py:87
  116.9 6.9 %copy-start.1 = (f32[6,224,1536]{2,1,0:T(8,128)S(1)}, f32[6,224,1536]{2,1,0:T(8,128)}, u32[]{:S(2)}) copy-start(f32[6,224,1536]{2,1,0:T(8,128)} %get-tuple-element.17) | copy-start | bytes 24772612
  118.7 5.1 %copy-start.5 = (f32[6,224]{1,0:T(8,128)S(1)}, f32[6,224]{1,0:T(8,128)}, u32[]{:S(2)}) copy-start(f32[6,224]{1,0:T(8,128)} %copy-done.4) | copy-start | bytes 16132
  122.3 1.6 copy-start.7
  126.2 2.0 copy-start.2
  130.5 66.6 %reduce-scatter.5.cloned.1.call-start = ((), (), s32[]{:S(2)}) async-start(), calls=%async_computation.4 | async-start | bytes 1032192 | tf_op jit(solution)/shard_map/reduce_scatter | solution.py:99
  131.2 50.6 %copy-start.6 = (f32[6,224]{1,0:T(8,128)S(1)}, f32[6,224]{1,0:T(8,128)}, u32[]{:S(2)}) copy-start(f32[6,224]{1,0:T(8,128)} %copy-done.4) | copy-start | bytes 16132
  181.8 5.5 %copy-start.3 = (bf16[6,224,1536]{2,1,0:T(8,128)(2,1)S(1)}, bf16[6,224,1536]{2,1,0:T(8,128)(2,1)}, u32[]{:S(2)}) copy-start(bf16[6,224,1536]{2,1,0:T(8,128)(2,1)} %copy-done.2) | copy-start | bytes 12386308
Sparse Core Ops, SparseCore 0:
  59.3 57.5 all-reduce.1
  130.6 29.8 reduce-scatter.2
  164.8 32.2 reduce-scatter.4
where the time goes:
time: 206 us; the launch traced here: 205 us
  waiting for transfers between devices  93.5 us (45%)
  blocking collectives  55.2 us (27%)
  matrix products  24.5 us (12%)
  between operations  13.9 us (7%)
  other arithmetic  13.1 us (6%)
  local copies, waits for them, and re-layouts  4.87 us (2%)
    psum x1, waiting for transfers between devices, body(): context = lax.psum(value_partial, 'frame')  57.4 us
    reduce_scatter x1, waiting for transfers between devices, body(): lax.psum_scatter(jnp.einsum('slf,fd->lsd', score_gradient, upstream_signa...  28.7 us
    psum x1, blocking collectives, body(): loss = lax.psum(jnp.sum(loss_part), 'rec')  17.1 us
    all_gather x1, blocking collectives, body(): lax.all_gather(texts, 'rec', axis=0, tiled=True)  16.6 us
    all_gather x1, blocking collectives, body(): query_vectors = lax.all_gather(local, 'frame', axis=1, tiled=True)  12.4 us
    pmax x1, blocking collectives, body(): row_max = lax.pmax(local_max, 'frame')  9.08 us
    reduce_scatter x1, waiting for transfers between devices, body(): lax.psum_scatter(text_term, 'rec', scatter_dimension=0, tiled=True)  7.46 us
    dot_general x1, matrix products, body(): jnp.einsum('pqx,xh->pqh', batch_weights, upstream_signal, preferred_eleme...  5.96 us
  transfers between devices with their start and end apart: 3, of which 3 were waited for; matrix products, arithmetic and copies ran while one was open for 5% of the time, Pallas kernels for 0%

commit v1 on v0

--- a/solution.py
+++ b/solution.py
@@ -69,7 +69,7 @@
     query_f = query_vectors.astype(jnp.float32)
     q_norm = lax.rsqrt(jnp.sum(query_f * query_f, axis=2) + EPS)
     q_unit = query_f * q_norm[..., None]
-    context = lax.psum(value_partial, "frame")
+    context = jax.lax.all_gather(value_partial, "frame").sum(axis=0)
     c_norm = lax.rsqrt(jnp.sum(context * context, axis=2) + EPS)
     c_unit = context * c_norm[..., None]
     cos = jnp.sum(q_unit * c_unit, axis=2)

time: 206 us -> 213 us (1.034)
  waiting for transfers between devices: 93.5 us -> 99.5 us
  matrix products: 24.5 us -> 26.7 us
    all_gather x0 -> x1, waiting for transfers between devices: none -> 63.4 us  [body(): context = jax.lax.all_gather(value_partial, 'frame').sum(axis=0)]
    psum x1 -> x0, waiting for transfers between devices: 57.4 us -> none  [body(): context = lax.psum(value_partial, 'frame')]
    reduce_sum x0 -> x1, other arithmetic: none -> 3.1 us  [body(): context = jax.lax.all_gather(value_partial, 'frame').sum(axis=0)]
    dot_general x1, matrix products: 2.32 us -> 4.58 us  [body(): jnp.einsum('ype,je->ypj', context_batch_gradient, upstream_signal, prefer...]
  transfers between devices with their start and end apart: 3 -> 3, of which waited for: 3 -> 3; matrix products, arithmetic and copies ran while one was open for 5% -> 4% of each run, Pallas kernels for 0% -> 0%
where the time goes in v1:
time: 213 us
  waiting for transfers between devices  99.5 us (47%)
  blocking collectives  55.2 us (26%)
  matrix products  26.7 us (13%)
  between operations  14 us (7%)
  other arithmetic  11.8 us (6%)
  local copies, waits for them, and re-layouts  5.28 us (2%)
    all_gather x1, waiting for transfers between devices, body(): context = jax.lax.all_gather(value_partial, 'frame').sum(axis=0)  63.4 us
    reduce_scatter x1, waiting for transfers between devices, body(): lax.psum_scatter(jnp.einsum('slf,fd->lsd', score_gradient, upstream_signa...  28.6 us
    psum x1, blocking collectives, body(): loss = lax.psum(jnp.sum(loss_part), 'rec')  17.1 us
    all_gather x1, blocking collectives, body(): lax.all_gather(texts, 'rec', axis=0, tiled=True)  16.6 us
    all_gather x1, blocking collectives, body(): query_vectors = lax.all_gather(local, 'frame', axis=1, tiled=True)  12.4 us
    pmax x1, blocking collectives, body(): row_max = lax.pmax(local_max, 'frame')  9.08 us
    reduce_scatter x1, waiting for transfers between devices, body(): lax.psum_scatter(text_term, 'rec', scatter_dimension=0, tiled=True)  7.46 us
    dot_general x1, matrix products, body(): jnp.einsum('pqx,xh->pqh', batch_weights, upstream_signal, preferred_eleme...  5.92 us
  transfers between devices with their start and end apart: 3, of which 3 were waited for; matrix products, arithmetic and copies ran while one was open for 4% of the time, Pallas kernels for 0%

profile of v1, /device:TPU:0, one launch (start us, length us, event | category | flops | bytes accessed | tf_op | source)
XLA Modules:
  0.0 212.6 jit_solution(7416174934776923223)
XLA Ops:
  7.2 0.0 copy-start
  7.2 0.0 all-gather.3.cloned.1.call-start
  7.2 0.7 multiply_add_fusion
  8.0 0.7 broadcast_compare_fusion.1
  8.6 0.9 select_reduce_fusion
  9.5 0.8 select_reduce_fusion.2
  10.3 0.0 copy-start.8
  10.4 0.0 copy-start.9
  10.4 16.6 %all_gather.12 = bf16[16,56,256]{2,1,0:T(8,128)(2,1)S(1)} all-gather(bf16[2,56,256]{2,1,0:T(8,128)(2,1)} %param.6), channel_id=1, replica_groups=mesh['rec'=8,'frame'=4] {'rec'}, dimensions={0}, use_global_device_ids=true | all-gather | bytes 516096 | tf_op jit(solution)/shard_map/all_gather | solution.py:50
  27.0 0.3 convolution_convert_fusion
  27.3 0.0 copy-done.8
  27.3 0.0 copy-done.9
  27.3 12.4 %all_gather.13 = bf16[6,224,256]{2,1,0:T(8,128)(2,1)S(1)} all-gather(bf16[6,56,256]{2,1,0:T(8,128)(2,1)S(1)} %copy.19), channel_id=1, replica_groups=mesh['rec'=8,'frame'=4] {'frame'}, dimensions={1}, use_global_device_ids=true | all-gather | bytes 860160 | tf_op jit(solution)/shard_map/all_gather | solution.py:53
  39.7 0.0 copy-done
  39.7 4.4 %multiply_reduce_fusion = (f32[6,224]{1,0:T(8,128)S(1)}, f32[6,224,1536]{2,1,0:T(8,128)}) fusion(bf16[6,224,256]{2,1,0:T(8,128)(2,1)S(1)} %all_gather.13, bf16[1,1536,256]{2,1,0:T(8,128)(2,1)S(1)} %copy-done), kind=kOutput, calls=%fused_computation.2 | convolution fusion | flops 1061092032 | bytes 9737472 | tf_op jit(solution)/shard_map/ype,je->ypj/dot_general | solution.py:57
  44.2 9.1 %pmax.7 = f32[6,224]{1,0:T(8,128)S(1)} all-reduce(f32[6,224]{1,0:T(8,128)S(1)} %get-tuple-element.16), channel_id=1, replica_groups=mesh['rec'=8,'frame'=4] {'frame'}, use_global_device_ids=true, to_apply=%region_6.0 | all-reduce | flops 1344 | bytes 10752 | tf_op jit(solution)/shard_map/pmax | solution.py:63
  53.2 0.0 copy-start.4
  53.3 5.9 %fusion.7 = f32[6,224,256]{2,1,0:T(8,128)} fusion(bf16[1,1536,256]{2,1,0:T(8,128)(2,1)S(1)} %copy-done, f32[6,224,1536]{2,1,0:T(8,128)} %get-tuple-element.17, f32[6,224]{1,0:T(8,128)S(1)} %pmax.7), kind=kOutput, calls=%fused_computation.18 | convolution fusion | flops 1063157760 | bytes 10425600 | tf_op jit(solution)/shard_map/pqx,xh->pqh/dot_general | solution.py:66
  59.2 0.0 copy-done.4
  59.2 0.0 all-gather.3.cloned.1.call-update
  59.2 0.0 reduce-scatter.3.cloned.1.call-start
  59.3 0.3 fusion.4
  59.6 63.4 %all-gather.3.cloned.1.call-done = f32[24,224,256]{2,1,0:T(8,128)} async-done(((f32[6,224,256]{2,1,0:T(8,128)}), f32[24,224,256]{2,1,0:T(8,128)}) %all-gather.3.cloned.1.call-update) | async-done | bytes 5505040 | tf_op jit(solution)/shard_map/all_gather | solution.py:72
  122.9 3.1 %reduce_sum.95 = f32[6,224,256]{2,1,0:T(8,128)S(1)} reduce(f32[4,6,224,256]{3,2,1,0:T(8,128)} %bitcast.43, f32[]{:T(128)} %constant.14.clone.1), dimensions={0}, to_apply=%region_7.0 | reduce | flops 1032192 | bytes 6881284 | tf_op jit(solution)/shard_map/reduce_sum | solution.py:72
  126.0 0.3 multiply_reduce_fusion.1
  126.3 0.0 copy-start.5
  126.4 0.8 multiply_reduce_fusion.2
  127.1 0.0 copy-start.1
  127.1 0.7 fusion.31
  127.9 0.0 copy-start.7
  127.9 0.4 copy-done.1
  128.3 0.7 convert_multiply_fusion
  129.0 0.0 copy-done.7
  129.0 0.0 copy-done.5
  129.0 4.6 %multiply_convert_fusion = bf16[6,224,1536]{2,1,0:T(8,128)(2,1)S(1)} fusion(f32[6,224,1536]{2,1,0:T(8,128)} %get-tuple-element.17, bf16[6,224,256]{2,1,0:T(8,128)(2,1)S(1)} %get-tuple-element.13, f32[6,224]{1,0:T(8,128)S(1)} %copy-done.5, bf16[1,1536,256]{2,1,0:T(8,128)(2,1)S(1)} %copy-done), kind=kOutput, calls=%fused_computation | convolution fusion | flops 1067286528 | bytes 13866240 | tf_op jit(solution)/shard_map/ype,je->ypj/dot_general | solution.py:83
  133.6 0.0 copy-start.2
  133.6 2.0 copy-done.2
  135.6 2.3 %convolution_bitcast_fusion.2 = f32[224,6,256]{2,0,1:T(8,128)} fusion(bf16[6,224,1536]{2,1,0:T(8,128)(2,1)S(1)} %multiply_convert_fusion, bf16[1,1536,256]{2,1,0:T(8,128)(2,1)S(1)} %copy-done), kind=kOutput, calls=%fused_computation.11 | convolution fusion | flops 1056964608 | bytes 6291456 | tf_op jit(solution)/shard_map/slf,fd->lsd/dot_general | solution.py:88
  137.9 0.0 reduce-scatter.3.cloned.1.call-update
  137.9 0.0 reduce-scatter.5.cloned.1.call-start
  138.0 0.7 constant_dynamic-slice_fusion
  138.7 0.0 copy-start.6
  138.7 0.7 constant_dynamic-slice_fusion.1
  139.3 28.6 %reduce-scatter.3.cloned.1.call-done = f32[56,6,256]{2,0,1:T(8,128)} async-done(((f32[224,6,256]{2,0,1:T(8,128)}), f32[56,6,256]{2,0,1:T(8,128)}) %reduce-scatter.3.cloned.1.call-update) | async-done | bytes 344080 | tf_op jit(solution)/shard_map/reduce_scatter | solution.py:87
  168.0 1.2 fusion.19
  169.2 1.4 fusion.13
  170.6 1.5 copy.21
  172.1 0.0 reduce-scatter.5.cloned.1.call-update
  172.1 17.1 %psum.7 = f32[]{:T(128)} all-reduce(f32[]{:T(128)} %get-tuple-element.15), channel_id=1, replica_groups=mesh['rec'=8,'frame'=4] {'rec'}, use_global_device_ids=true, to_apply=%region_11.12 | all-reduce | flops 1 | bytes 8 | tf_op jit(solution)/shard_map/psum | solution.py:109
  189.2 0.0 copy-done.6
  189.2 0.0 copy-start.3
  189.2 5.5 %convolution_bitcast_fusion = f32[1536,256]{1,0:T(8,128)S(1)} fusion(bf16[6,224,256]{2,1,0:T(8,128)(2,1)S(1)} %get-tuple-element.13, f32[6,224,1536]{2,1,0:T(8,128)} %get-tuple-element.17, f32[6,224]{1,0:T(8,128)S(1)} %copy-done.6), kind=kOutput, calls=%fused_computation.4 | convolution fusion | flops 1063157760 | bytes 10523904 | tf_op jit(solution)/shard_map/cvm,cvz->mz/dot_general | solution.py:105
  194.7 0.0 copy-done.3
  194.7 2.4 %fusion.3 = bf16[1,1536,256]{2,1,0:T(8,128)(2,1)} fusion(f32[1536,256]{1,0:T(8,128)S(1)} %convolution_bitcast_fusion, bf16[6,224,1536]{2,1,0:T(8,128)(2,1)S(1)} %copy-done.3, bf16[6,224,256]{2,1,0:T(8,128)(2,1)S(1)} %all_gather.13), kind=kOutput, calls=%fused_computation.8 | convolution fusion | flops 1057751040 | bytes 7176192 | tf_op jit(solution)/shard_map/cvm,cvz->mz/dot_general | solution.py:102
  197.1 7.5 %reduce-scatter.5.cloned.1.call-done = f32[2,56,256]{2,1,0:T(8,128)} async-done(((f32[16,56,256]{2,1,0:T(8,128)}), f32[2,56,256]{2,1,0:T(8,128)}) %reduce-scatter.5.cloned.1.call-update) | async-done | bytes 114704 | tf_op jit(solution)/shard_map/reduce_scatter | solution.py:99
  204.6 1.5 convert_element_type.54
  (4 shorter events, 0.0 us)
Async XLA Ops:
  7.2 32.6 %copy-start = (bf16[1,1536,256]{2,1,0:T(8,128)(2,1)S(1)}, bf16[1,1536,256]{2,1,0:T(8,128)(2,1)}, u32[]{:S(2)}) copy-start(bf16[1,1536,256]{2,1,0:T(8,128)(2,1)} %param.5) | copy-start | bytes 2359300
  7.2 115.8 %all-gather.3.cloned.1.call-start = ((), (), s32[]{:S(2)}) async-start(), calls=%async_computation.4 | async-start | bytes 6881280 | tf_op jit(solution)/shard_map/all_gather | solution.py:72
  10.3 16.9 %copy-start.8 = (s32[6]{0:T(128)}, s32[6]{0:T(128)S(1)}, u32[]{:S(2)}) copy-start(s32[6]{0:T(128)S(1)} %get-tuple-element.9) | copy-start | bytes 76
  10.4 16.9 %copy-start.9 = (pred[6]{0:T(512)(128)(4,1)}, pred[6]{0:T(512)(128)(4,1)S(1)}, u32[]{:S(2)}) copy-start(pred[6]{0:T(512)(128)(4,1)S(1)} %broadcast_compare_fusion) | copy-start | bytes 22
  53.2 5.9 %copy-start.4 = (f32[6,224]{1,0:T(8,128)}, f32[6,224]{1,0:T(8,128)S(1)}, u32[]{:S(2)}) copy-start(f32[6,224]{1,0:T(8,128)S(1)} %pmax.7) | copy-start | bytes 16132
  59.2 108.8 %reduce-scatter.3.cloned.1.call-start = ((), (), s32[]{:S(2)}) async-start(), calls=%async_computation.2 | async-start | bytes 1720320 | tf_op jit(solution)/shard_map/reduce_scatter | solution.py:87
  126.3 2.7 %copy-start.5 = (f32[6,224]{1,0:T(8,128)S(1)}, f32[6,224]{1,0:T(8,128)}, u32[]{:S(2)}) copy-start(f32[6,224]{1,0:T(8,128)} %copy-done.4) | copy-start | bytes 16132
  127.1 1.2 copy-start.1
  127.9 1.1 copy-start.7
  133.6 2.0 copy-start.2
  137.9 66.7 %reduce-scatter.5.cloned.1.call-start = ((), (), s32[]{:S(2)}) async-start(), calls=%async_computation.3 | async-start | bytes 1032192 | tf_op jit(solution)/shard_map/reduce_scatter | solution.py:99
  138.7 50.6 %copy-start.6 = (f32[6,224]{1,0:T(8,128)S(1)}, f32[6,224]{1,0:T(8,128)}, u32[]{:S(2)}) copy-start(f32[6,224]{1,0:T(8,128)} %copy-done.4) | copy-start | bytes 16132
  189.2 5.5 %copy-start.3 = (bf16[6,224,1536]{2,1,0:T(8,128)(2,1)S(1)}, bf16[6,224,1536]{2,1,0:T(8,128)(2,1)}, u32[]{:S(2)}) copy-start(bf16[6,224,1536]{2,1,0:T(8,128)(2,1)} %copy-done.2) | copy-start | bytes 12386308
Sparse Core Ops, SparseCore 0:
  59.3 63.5 all-gather.2
  138.1 29.8 reduce-scatter.2
  172.2 32.3 reduce-scatter.4
